TPU v7x, 32 devices: a whole 2x2x4 slice. The times are simulated.
32 devices in a mesh: seq: 4 (over x, core), head: 8 (over z, y).
Axes of the slice: x: 2, y: 2, z: 4, core: 2. Of those that a mesh axis runs over, the one named last changes fastest.
Arguments:
- features: bfloat16 [16384, 12288], P(('seq', 'head')), may hold values from -6 to 6
- selector: bfloat16 [16384, 256], P(('seq', 'head')), may hold values from -6 to 6
- step_input: bfloat16 [16384, 96], P(('seq', 'head')), may hold values from -2 to 20
- feature_kernel: float32 [4, 12288], replicated, may hold values from -3 to 3
- selector_kernel: float32 [4, 256], replicated, may hold values from -3 to 3
- feature_offset: float32 [12288], replicated, may hold values from -3 to 3
- selector_offset: float32 [256], replicated, may hold values from -3 to 3
- decay_log: float32 [96], replicated, may hold values from -2.4 to 0.1
- step_offset: float32 [96], replicated, may hold values from -12 to -2
- skip_scale: float32 [96], replicated, may hold values from 0.5 to 1.5
- norm_gain: float32 [12288], replicated, may hold values from 0.5 to 1.5
Outputs:
- output: bfloat16 [16384, 12288], P(('seq', 'head'))
All inputs are finite; a program needn't handle non-finite values.
Results may differ from a plain program's by a relative error of at most 0.008.
Values may be sent and summed in bfloat16 or wider, within the bound.
No kernel may reach another device: no remote copies, remote signals or barrier semaphores. Data moves between devices by JAX's collectives and lax.ppermute only.
A program may use at most 192 MiB of HBM per device.

v0:
```python
import math

import jax
import jax.numpy as jnp
from jax import lax
from jax.sharding import PartitionSpec as P

SPAN = 256


def passed_along(shard, axis, by):
    peers = lax.axis_size(axis)
    pairs = [(i, i + by) for i in range(peers) if 0 <= i + by < peers]
    return lax.ppermute(shard, axis, pairs)


def entering_2(shard, axis, join, neutral):
    place = lax.axis_index(axis)
    gathered = jax.tree.map(
        lambda a, kind: lax.all_gather(a.astype(kind), axis), shard, (jnp.bfloat16, jnp.bfloat16)
    )
    state = jax.tree.map(lambda a, e: jnp.zeros_like(a) + jnp.asarray(e, a.dtype), shard, neutral)

    def one(turn, state):
        return join(
            state,
            jax.tree.map(
                lambda a, own: lax.dynamic_index_in_dim(a, turn, 0, False).astype(own.dtype),
                gathered,
                shard,
            ),
        )

    return lax.fori_loop(0, place, one, state)


def causal_filter(tail_rows, new_rows, kernel, offset):
    length = new_rows.shape[0]
    window = jnp.concatenate([tail_rows, new_rows], axis=0).astype(jnp.float32)
    summed = jnp.broadcast_to(offset[None, :], (length, offset.shape[0]))
    for delay_step in range(kernel.shape[0]):
        summed = summed + kernel[delay_step][None, :] * window[delay_step : delay_step + length]
    return jax.nn.silu(summed).astype(jnp.bfloat16)


def normalize(values, norm_gain):
    widened = values.astype(jnp.float32)
    square = jnp.mean(widened * widened, axis=-1, keepdims=True)
    return (widened * lax.rsqrt(square + 1e-05) * norm_gain[None, :]).astype(jnp.bfloat16)


def join_states(former, latter):
    return (former[0] + latter[0], jnp.exp(latter[0])[:, None, None] * former[1] + latter[1])


def span_terms(feature_matrix_rows, write_rows, read_rows, step_size, log_decay):
    length = feature_matrix_rows.shape[0]
    head_count = step_size.shape[1]
    head_view = feature_matrix_rows.reshape(length, head_count, -1)
    cumulative = jnp.cumsum(log_decay, axis=0)
    inputs = (step_size[:, :, None] * head_view).astype(jnp.bfloat16)
    scores = jnp.dot(read_rows, write_rows.T, preferred_element_type=jnp.float32)
    log_spacing = cumulative.T[:, :, None] - cumulative.T[:, None, :]
    causal = jnp.arange(length)[:, None] >= jnp.arange(length)[None, :]
    decay_mask = jnp.exp(jnp.where(causal[None], log_spacing, -jnp.inf))
    mixing = (scores[None] * decay_mask).astype(jnp.bfloat16)
    diagonal = jnp.einsum("hij,jhp->ihp", mixing, inputs, preferred_element_type=jnp.float32)
    log_total = cumulative[-1]
    weighted = (
        (step_size * jnp.exp(log_total[None, :] - cumulative))[:, :, None] * head_view
    ).astype(jnp.bfloat16)
    span_state = jnp.einsum("jn,jhp->hnp", write_rows, weighted, preferred_element_type=jnp.float32)
    return (diagonal, cumulative, span_state, log_total)


def group_spans(values, span_count, group_size):
    return values.reshape((span_count // group_size, group_size, SPAN) + values.shape[1:])


def ungroup(values, span_count):
    return values.reshape((span_count,) + values.shape[2:])


def chain_states(span_states, log_totals):

    def advance(running, record):
        span_state, log_total = record
        return (jnp.exp(log_total)[:, None, None] * running + span_state, running)

    final_state, entering = lax.scan(
        advance, jnp.zeros_like(span_states[0]), (span_states, log_totals)
    )
    before = jnp.cumsum(log_totals, axis=0) - log_totals
    return (entering, before, final_state, jnp.sum(log_totals, axis=0))


def selective_rows(
    feature_conv, selector_conv, step_rows, decay_log, step_offset, skip_scale, carry_fn
):
    state_size = selector_conv.shape[1] // 2
    row_count = feature_conv.shape[0]
    span_count = row_count // SPAN
    group_size = math.gcd(span_count, 8)
    step_size = jax.nn.softplus(step_rows.astype(jnp.float32) + step_offset[None, :])
    log_decay = -jnp.exp(decay_log)[None, :] * step_size
    feature_groups = group_spans(feature_conv, span_count, group_size)
    read_groups = group_spans(selector_conv[:, state_size:], span_count, group_size)
    write_groups = group_spans(selector_conv[:, :state_size], span_count, group_size)

    def run_terms(group_items):
        return jax.vmap(span_terms)(*group_items)

    pieces = (
        feature_groups,
        write_groups,
        read_groups,
        group_spans(step_size, span_count, group_size),
        group_spans(log_decay, span_count, group_size),
    )
    diagonal, cumulative, span_states, log_totals = lax.map(run_terms, pieces)
    span_states = ungroup(span_states, span_count)
    log_totals = ungroup(log_totals, span_count)
    entering, before, final_state, block_log = chain_states(span_states, log_totals)
    state_in = carry_fn(block_log, final_state)

    def one_span(diag_rows, cumul_rows, read_rows, state_local, log_before, feature_matrix_rows):
        length, head_count, head_width = diag_rows.shape
        entry_state = state_local + jnp.exp(log_before)[:, None, None] * state_in
        carried = jnp.einsum(
            "in,hnp->ihp",
            read_rows,
            entry_state.astype(jnp.bfloat16),
            preferred_element_type=jnp.float32,
        )
        head_view = feature_matrix_rows.reshape(length, head_count, head_width).astype(jnp.float32)
        summed = (
            diag_rows
            + jnp.exp(cumul_rows)[:, :, None] * carried
            + skip_scale[None, :, None] * head_view
        )
        return summed.reshape(length, head_count * head_width).astype(jnp.bfloat16)

    def run_output(group_items):
        return jax.vmap(one_span)(*group_items)

    regroup_entering = entering.reshape((span_count // group_size, group_size) + entering.shape[1:])
    regroup_before = before.reshape((span_count // group_size, group_size) + before.shape[1:])
    results = lax.map(
        run_output,
        (diagonal, cumulative, read_groups, regroup_entering, regroup_before, feature_groups),
    )
    return results.reshape(row_count, -1)


def token_conv(
    features, selector, feature_kernel, selector_kernel, feature_offset, selector_offset
):
    tail_count = feature_kernel.shape[0] - 1
    channels = features.shape[1]
    row_count = features.shape[0]
    last_rows = jnp.concatenate(
        [features[row_count - tail_count :], selector[row_count - tail_count :]], axis=1
    )
    tail_rows = passed_along(last_rows, ("seq", "head"), 1)
    feature_conv = causal_filter(tail_rows[:, :channels], features, feature_kernel, feature_offset)
    selector_conv = causal_filter(
        tail_rows[:, channels:], selector, selector_kernel, selector_offset
    )
    return (feature_conv, selector_conv)


def on_device(
    features,
    selector,
    step_input,
    feature_kernel,
    selector_kernel,
    feature_offset,
    selector_offset,
    decay_log,
    step_offset,
    skip_scale,
    norm_gain,
):
    head_count = decay_log.shape[0] // lax.axis_size("head")
    head_first = lax.axis_index("head") * head_count
    feature_send, selector_send = token_conv(
        features, selector, feature_kernel, selector_kernel, feature_offset, selector_offset
    )
    feature_slab, step_slab = (
        lax.all_to_all(feature_send, "head", split_axis=1, concat_axis=0, tiled=True),
        lax.all_to_all(step_input, "head", split_axis=1, concat_axis=0, tiled=True),
    )
    selector_slab = lax.all_gather(selector_send, "head", axis=0, tiled=True)
    feature_conv, selector_conv = (feature_slab, selector_slab)
    own_decay = lax.dynamic_slice_in_dim(decay_log, head_first, head_count, axis=0)
    own_step = lax.dynamic_slice_in_dim(step_offset, head_first, head_count, axis=0)
    own_skip = lax.dynamic_slice_in_dim(skip_scale, head_first, head_count, axis=0)

    def slab_prefix(block_log, final_state):
        prefix = entering_2(
            (block_log, final_state),
            "seq",
            join_states,
            (jnp.zeros_like(block_log), jnp.zeros_like(final_state)),
        )
        return prefix[1]

    mixed = selective_rows(
        feature_conv, selector_conv, step_slab, own_decay, own_step, own_skip, slab_prefix
    )
    blended_rows = lax.all_to_all(mixed, "head", split_axis=0, concat_axis=1, tiled=True)
    return normalize(blended_rows, norm_gain)


def solution(mesh):
    placed = (
        P(("seq", "head"), None),
        P(("seq", "head"), None),
        P(("seq", "head"), None),
        P(),
        P(),
        P(),
        P(),
        P(),
        P(),
        P(),
        P(),
    )
    return jax.shard_map(
        on_device, mesh=mesh, in_specs=placed, out_specs=P(("seq", "head"), None), check_vma=False
    )
```

profile of v0, /device:TPU:0, one launch (start us, length us, event | category | flops | bytes accessed | tf_op | source)
XLA Modules:
  0.0 1044.4 jit_solution(126070698641346954)
XLA Ops:
  8.1 7.3 all-to-all-start
  23.3 16.6 %copy.85 = bf16[512,12288]{0,1:T(8,128)(2,1)} copy(bf16[512,12288]{1,0:T(8,128)(2,1)} %param.19) | data formatting | bytes 25165824 | tf_op args[0]
  42.2 17.2 %maximum_convert_fusion = f32[515,12288]{0,1:T(8,128)} fusion(bf16[512,12288]{0,1:T(8,128)(2,1)} %copy.85, bf16[3,12288]{0,1:T(8,128)(2,1)S(1)} %copy.84), kind=kLoop, calls=%fused_computation.78 | loop fusion | flops 25313280 | bytes 37969920 | tf_op jit(solution)/shard_map/convert_element_type | solution.py:39
  59.4 59.4 %multiply_convert_fusion.4 = bf16[512,12288]{0,1:T(8,128)(2,1)} fusion(f32[515,12288]{0,1:T(8,128)} %maximum_convert_fusion, f32[12288]{0:T(1024)S(1)} %bitcast.193, f32[12288]{0:T(1024)S(1)} %bitcast.194, f32[12288]{0:T(1024)S(1)} %bitcast.192, f32[12288]{0:T(1024)S(1)} %bitcast.191, f32[12288]{0:T(1024)S(1)} %copy-done.10), kind=kLoop, calls=%fused_computation.77 | loop fusion | flops 81788928 | bytes 113491968 | tf_op jit(solution)/shard_map/convert_element_type | solution.py:43
  127.2 237.7 %all-gather.5.cloned.1.call-done = bf16[4096,256]{1,0:T(8,128)(2,1)} async-done(((bf16[512,256]{1,0:T(8,128)(2,1)}), bf16[4096,256]{1,0:T(8,128)(2,1)}) %all-gather.5.cloned.1.call-update) | async-done | bytes 2097168 | tf_op jit(solution)/shard_map/all_gather | solution.py:194
  366.6 55.9 %all-to-all-done.1 = bf16[512,8,1536]{0,2,1:T(8,128)(2,1)} async-done(((bf16[512,8,1536]{0,2,1:T(8,128)(2,1)}), bf16[512,8,1536]{0,2,1:T(8,128)(2,1)}, u32[]{:S(2)}, u32[]{:S(2)}) %all-to-all-start.1) | async-done | bytes 12582944 | tf_op jit(solution)/shard_map/all_to_all | solution.py:191
  422.5 16.7 %copy.86 = bf16[8,512,1536]{2,1,0:T(8,128)(2,1)} copy(bf16[8,512,1536]{1,2,0:T(8,128)(2,1)} %bitcast.40) | data formatting | bytes 25165824 | tf_op jit(solution)/shard_map/all_to_all | solution.py:191
  439.2 15.7 %copy.89 = bf16[2,8,256,1536]{2,3,1,0:T(8,128)(2,1)} copy(bf16[2,8,256,1536]{3,2,1,0:T(8,128)(2,1)} %bitcast.181) | data formatting | bytes 25165824 | tf_op jit(solution)/shard_map/while | solution.py:120
  454.9 76.1 %while.51 = (s32[]{:T(128)}, f32[2,8,256,12,128]{2,4,3,1,0:T(8,128)}, f32[2,8,256,12]{2,1,3,0:T(8,128)}, f32[2,8,12,128,128]{4,3,2,1,0:T(8,128)}, f32[2,8,12]{2,...) while((s32[]{:T(128)}, ...), condition=%wide.region_3.4_spmd, body=%wide.region_0.3_spmd.sunk | while | flops 2597437696 | bytes 77813640 | solution.py:120
  465.0 9.7 bitcast_dynamic-update-slice_fusion.8
  479.3 6.5 copy.142
  485.8 6.3 constant_dynamic-update-slice_fusion.4
  503.1 9.7 bitcast_dynamic-update-slice_fusion.8
  517.3 6.5 copy.142
  523.8 6.3 constant_dynamic-update-slice_fusion.4
  530.9 36.3 %while.54 = (s32[]{:T(128)}, f32[12,128,128]{2,1,0:T(8,128)S(1)}, f32[16,12,128,128]{3,2,1,0:T(8,128)}, f32[16,12]{1,0:T(8,128)S(1)}, f32[16,12,128,128]{3,2,1,0:T(8,128)}, /*index=5*/s32[]{:T(128)}, s32[]{:T(128)}) while((s32[]{:T(128)}, f32[12,128,128]{2,1,0:T(8,128)S(1)}, f32[16,12,128,128]{3,2,1,0:T(8,128)}, ...), condition=%wide.region_5.6_spmd.clone, body=%wide.region_4.5_spmd.clone.sunk | while | flops 786435 | bytes 3932912 | solution.py:90
  575.5 11.0 %all-gather.7.cloned.1.call-done = bf16[48,128,128]{2,1,0:T(8,128)(2,1)} async-done(((bf16[12,128,128]{2,1,0:T(8,128)(2,1)}), bf16[48,128,128]{2,1,0:T(8,128)(2,1)}) %all-gather.7.cloned.1.call-update) | async-done | bytes 1572880 | tf_op jit(solution)/shard_map/all_gather | solution.py:20
  587.0 94.6 %while.53 = (s32[]{:T(128)}, bf16[2,8,256,1536]{3,2,1,0:T(8,128)(2,1)}, f32[2,8,256,12,128]{2,4,3,1,0:T(8,128)}, f32[2,8,256,12]{2,1,3,0:T(8,128)S(1)}, bf16[2,8...) while((s32[]{:T(128)}, ...), condition=%wide.region_11.12_spmd, body=%wide.region_10.11_spmd.sunk | while | flops 828899328 | bytes 142313392 | solution.py:148
  587.0 6.9 constant_dynamic-slice_fusion.11
  593.9 6.5 copy.145
  609.1 10.5 %fusion.86 = bf16[8,256,12,128]{1,3,2,0:T(8,128)(2,1)} fusion(bf16[8,256,12,128]{1,3,2,0:T(8,128)(2,1)S(1)} %bitcast.176, f32[8,256,12,128]{1,3,2,0:T(8,128)S(1)} %bitcast.173, f32[2,8,256,12,128]{2,4,3,1,0:T(8,128)} %get-tuple-element.654, s32[]{:T(128)} %get-tuple-element.641, f32[12]{0:T(128)S(1)} %get-tuple-element.660, f32[8,256,12]{1,2,0:T(8,128)S(1)} %fusion.85), kind=kLoop, calls=%fused_computation.43.clone.1 | loop fusion | flops 18874368 | bytes 37847092 | tf_op jit(solution)/shard_map/while/body/eval_jaxpr/vmap()/convert_element_type | solution.py:141
  619.6 8.8 copy.146
  634.3 6.9 constant_dynamic-slice_fusion.11
  641.2 6.5 copy.145
  656.4 10.5 %fusion.86 = bf16[8,256,12,128]{1,3,2,0:T(8,128)(2,1)} fusion(bf16[8,256,12,128]{1,3,2,0:T(8,128)(2,1)S(1)} %bitcast.176, f32[8,256,12,128]{1,3,2,0:T(8,128)S(1)} %bitcast.173, f32[2,8,256,12,128]{2,4,3,1,0:T(8,128)} %get-tuple-element.654, s32[]{:T(128)} %get-tuple-element.641, f32[12]{0:T(128)S(1)} %get-tuple-element.660, f32[8,256,12]{1,2,0:T(8,128)S(1)} %fusion.85), kind=kLoop, calls=%fused_computation.43.clone.1 | loop fusion | flops 18874368 | bytes 37847092 | tf_op jit(solution)/shard_map/while/body/eval_jaxpr/vmap()/convert_element_type | solution.py:141
  666.9 8.8 copy.146
  681.6 279.6 %all_to_all.42 = bf16[8,512,1536]{2,1,0:T(8,128)(2,1)S(1)} all-to-all(bf16[8,512,1536]{2,1,0:T(8,128)(2,1)} %bitcast.187), channel_id=1, replica_groups=mesh['seq'=4,'head'=8] {'head'}, dimensions={0} | all-to-all | bytes 25165824 | tf_op jit(solution)/shard_map/all_to_all | solution.py:212
  966.0 9.4 convert_bitcast_fusion
  975.4 24.7 %copy.97 = f32[512,8,1536]{0,2,1:T(8,128)} copy(f32[512,8,1536]{2,0,1:T(8,128)} %convert_bitcast_fusion) | data formatting | bytes 50331648 | tf_op jit(solution)/shard_map/convert_element_type | solution.py:47
  1000.1 7.1 fusion.40
  1007.2 13.7 %fusion.46 = bf16[512,12288]{0,1:T(8,128)(2,1)} fusion(f32[512,8,1536]{0,2,1:T(8,128)} %copy.97, f32[12288]{0:T(1024)S(1)} %copy-done.11, f32[512]{0:T(512)S(1)} %add_rsqrt_fusion), kind=kLoop, calls=%fused_computation.76 | loop fusion | flops 18874368 | bytes 37799936 | tf_op jit(solution)/shard_map/convert_element_type | solution.py:49
  1020.9 16.6 %copy.98 = bf16[512,12288]{1,0:T(8,128)(2,1)} copy(bf16[512,12288]{0,1:T(8,128)(2,1)} %fusion.46) | data formatting | bytes 25165824 | tf_op jit(solution)/shard_map/convert_element_type | solution.py:49
  (199 shorter events, 130.3 us)
Async XLA Ops:
  8.1 110.7 %all-to-all-start = ((bf16[512,8,12]{0,2,1:T(8,128)(2,1)}), bf16[512,8,12]{0,2,1:T(8,128)(2,1)S(1)}, u32[]{:S(2)}, u32[]{:S(2)}) async-start(bf16[512,8,12]{0,2,1:T(8,128)(2,1)} %all_to_all.32), calls=%async_computation | async-start | bytes 262144 | tf_op jit(solution)/shard_map/all_to_all | solution.py:192
  17.1 22.8 %collective-permute-start = (bf16[3,12544]{1,0:T(4,128)(2,1)S(1)}, bf16[3,12544]{1,0:T(4,128)(2,1)S(1)}, u32[]{:S(2)}, u32[]{:S(2)}) collective-permute-start(bf16[3,12544]{1,0:T(4,128)(2,1)S(1)} %pad_maximum_fusion), channel_id=1, source_target_pairs={{0,1},{1,2},{2,3},{3,4},{4,5},{5,6},{6,7},{7,8},{8,9},{9,10},{10,1... | collective-permute-start | bytes 225800 | tf_op jit(solution)/shard_map/ppermute | solution.py:14
  39.9 0.6 copy-start.9
  42.2 17.2 %copy-start.8 = (f32[1,12288]{1,0:T(1,128)S(1)}, f32[1,12288]{1,0:T(1,128)}, u32[]{:S(2)}) copy-start(f32[1,12288]{1,0:T(1,128)} %get-tuple-element.351) | copy-start | bytes 147460
  42.2 17.2 %copy-start.10 = (f32[12288]{0:T(1024)S(1)}, f32[12288]{0:T(1024)}, u32[]{:S(2)}) copy-start(f32[12288]{0:T(1024)} %param.24) | copy-start | bytes 147460
  118.8 5.7 copy-start.12
  118.8 5.7 copy-start.7
  118.8 5.7 slice-start
  118.8 5.7 copy-start.13
  118.9 7.1 copy-start.14
  118.9 7.2 copy-start.15
  118.9 303.7 %all-to-all-start.1 = ((bf16[512,8,1536]{0,2,1:T(8,128)(2,1)}), bf16[512,8,1536]{0,2,1:T(8,128)(2,1)}, u32[]{:S(2)}, u32[]{:S(2)}) async-start(bf16[512,8,1536]{0,2,1:T(8,128)(2,1)} %bitcast.180), calls=%async_computation.1 | async-start | bytes 25165824 | tf_op jit(solution)/shard_map/all_to_all | solution.py:191
  124.4 240.6 %all-gather.5.cloned.1.call-start = ((), (), s32[]{:S(2)}) async-start(), calls=%async_computation.3 | async-start | bytes 2359296 | tf_op jit(solution)/shard_map/all_gather | solution.py:194
  125.7 460.7 %all-gather.7.cloned.1.call-start = ((), (), s32[]{:S(2)}) async-start(), calls=%async_computation.4 | async-start | bytes 1966080 | tf_op jit(solution)/shard_map/all_gather | solution.py:20
  454.9 76.1 %copy-start.1 = (f32[12,128,128]{2,1,0:T(8,128)S(1)}, f32[12,128,128]{2,1,0:T(8,128)}, u32[]{:S(2)}) copy-start(f32[12,128,128]{2,1,0:T(8,128)} %custom-call) | copy-start | bytes 2359300
  530.9 37.2 %copy-start.16 = (f32[96]{0:T(128)S(1)}, f32[96]{0:T(128)}, u32[]{:S(2)}) copy-start(f32[96]{0:T(128)} %param.28) | copy-start | bytes 1156
  530.9 37.2 %copy-start.17 = (u32[32]{0:T(128)S(1)}, u32[32]{0:T(128)}, u32[]{:S(2)}) copy-start(u32[32]{0:T(128)} %constant.111) | copy-start | bytes 388
  530.9 56.1 %copy-start.6 = (f32[2,8,256,12]{2,1,3,0:T(8,128)S(1)}, f32[2,8,256,12]{2,1,3,0:T(8,128)}, u32[]{:S(2)}) copy-start(f32[2,8,256,12]{2,1,3,0:T(8,128)} %get-tuple-element.633) | copy-start | bytes 589828
  587.0 13.4 %copy-start.4 = (f32[12,128,128]{1,2,0:T(8,128)}, f32[12,128,128]{1,2,0:T(8,128)S(1)}, u32[]{:S(2)}) copy-start(f32[12,128,128]{1,2,0:T(8,128)S(1)} %get-tuple-element.659) | copy-start | bytes 2359300 | tf_op jit(solution)/shard_map/while
  587.0 17.0 %copy-start.2 = (bf16[2,8,256,128]{3,2,1,0:T(8,128)(2,1)}, bf16[2,8,256,128]{3,2,1,0:T(8,128)(2,1)S(1)}, u32[]{:S(2)}) copy-start(bf16[2,8,256,128]{3,2,1,0:T(8,128)(2,1)S(1)} %get-tuple-element.656) | copy-start | bytes 3145732 | tf_op jit(solution)/shard_map/while
  619.6 14.7 %copy-start.3 = (bf16[2,8,256,128]{3,2,1,0:T(8,128)(2,1)S(1)}, bf16[2,8,256,128]{3,2,1,0:T(8,128)(2,1)}, u32[]{:S(2)}) copy-start(bf16[2,8,256,128]{3,2,1,0:T(8,128)(2,1)} %copy-done.2) | copy-start | bytes 3145732 | tf_op jit(solution)/shard_map/while
  619.6 14.7 %copy-start.5 = (f32[12,128,128]{1,2,0:T(8,128)S(1)}, f32[12,128,128]{1,2,0:T(8,128)}, u32[]{:S(2)}) copy-start(f32[12,128,128]{1,2,0:T(8,128)} %copy-done.4) | copy-start | bytes 2359300 | tf_op jit(solution)/shard_map/while
  634.3 13.4 %copy-start.4 = (f32[12,128,128]{1,2,0:T(8,128)}, f32[12,128,128]{1,2,0:T(8,128)S(1)}, u32[]{:S(2)}) copy-start(f32[12,128,128]{1,2,0:T(8,128)S(1)} %get-tuple-element.659) | copy-start | bytes 2359300 | tf_op jit(solution)/shard_map/while
  634.3 17.0 %copy-start.2 = (bf16[2,8,256,128]{3,2,1,0:T(8,128)(2,1)}, bf16[2,8,256,128]{3,2,1,0:T(8,128)(2,1)S(1)}, u32[]{:S(2)}) copy-start(bf16[2,8,256,128]{3,2,1,0:T(8,128)(2,1)S(1)} %get-tuple-element.656) | copy-start | bytes 3145732 | tf_op jit(solution)/shard_map/while
  666.9 14.7 %copy-start.3 = (bf16[2,8,256,128]{3,2,1,0:T(8,128)(2,1)S(1)}, bf16[2,8,256,128]{3,2,1,0:T(8,128)(2,1)}, u32[]{:S(2)}) copy-start(bf16[2,8,256,128]{3,2,1,0:T(8,128)(2,1)} %copy-done.2) | copy-start | bytes 3145732 | tf_op jit(solution)/shard_map/while
  666.9 14.7 %copy-start.5 = (f32[12,128,128]{1,2,0:T(8,128)S(1)}, f32[12,128,128]{1,2,0:T(8,128)}, u32[]{:S(2)}) copy-start(f32[12,128,128]{1,2,0:T(8,128)} %copy-done.4) | copy-start | bytes 2359300 | tf_op jit(solution)/shard_map/while
  961.2 4.8 copy-start
  1000.1 7.1 copy-start.11
Sparse Core Ops, SparseCore 0:
  127.3 237.5 all-gather.4
  568.2 18.1 all-gather.6
where the time goes:
time: 1050 us; the launch traced here: 1040 us
  waiting for transfers between devices  305 us (29%)
  blocking collectives  285 us (27%)
  local copies, waits for them, and re-layouts  204 us (19%)
  other arithmetic  185 us (18%)
  matrix products  32.8 us (3%)
  starting transfers between devices  17 us (2%)
  between operations  14.4 us (1%)
    all_to_all x1, blocking collectives, on_device(): lax.all_to_all(mixed, 'head', split_axis=0, concat_axis=1, tiled=True)  280 us
    all_gather x1, waiting for transfers between devices, on_device(): selector_slab = lax.all_gather(selector_send, 'head', axis=0, tiled=True)  238 us
    convert_element_type x2, other arithmetic, causal_filter(): return jax.nn.silu(summed).astype(jnp.bfloat16)  60.5 us
    all_to_all x1, waiting for transfers between devices, on_device(): lax.all_to_all(feature_send, 'head', split_axis=1, concat_axis=0, tiled=T...  55.9 us
    dynamic_update_slice x4, local copies, waits for them, and re-layouts, selective_rows(): lax.map(run_output, (diagonal, cumulative, read_groups, regroup_entering,...  29.4 us
    dynamic_update_slice x8, local copies, waits for them, and re-layouts, selective_rows(): diagonal, cumulative, span_states, log_totals = lax.map(run_terms, pieces)  27 us
    dynamic_slice x4, local copies, waits for them, and re-layouts, selective_rows(): lax.map(run_output, (diagonal, cumulative, read_groups, regroup_entering,...  26.8 us
    convert_element_type x1, local copies, waits for them, and re-layouts, normalize(): widened = values.astype(jnp.float32)  24.7 us
  transfers between devices with their start and end apart: 5, of which 3 were waited for; matrix products, arithmetic and copies ran while one was open for 10% of the time, Pallas kernels for 0%

commit v1 on v0

v1 whole, which is shorter than its diff:
```python
import functools

import jax
import jax.numpy as jnp
from jax import lax
from jax.experimental import pallas as pl
from jax.experimental.pallas import tpu as pltpu
from jax.sharding import Mesh, PartitionSpec as P

SPAN = 256
LANES = 128
LOG2E = 1.4426950408889634
BF16 = jnp.bfloat16
F32 = jnp.float32
SMEM = pltpu.MemorySpace.SMEM
VMEM = pltpu.MemorySpace.VMEM
ALL = ("seq", "pair", "side")
GROUP = ("seq", "pair")


def dot(a, b):
    return jnp.dot(a, b, preferred_element_type=F32)


def cost(flops, nbytes):
    return pl.CostEstimate(flops=int(flops), bytes_accessed=int(nbytes), transcendentals=0)


def whole_vmem(n):
    return [pl.BlockSpec(memory_space=VMEM)] * n


def rates_kernel(step_ref, off_ref, dlog_ref, dt_ref, wst_ref, cum_ref, cumt_ref, ecum_ref, edev_ref, tot_ref, last_ref):
    rows, heads = step_ref.shape
    spans = rows // SPAN
    for ref in (dt_ref, wst_ref, cum_ref, ecum_ref, edev_ref):
        ref[...] = jnp.zeros_like(ref)
    raw = step_ref[...].astype(F32) + off_ref[...]
    step = jnp.maximum(raw, 0.0) + jnp.log1p(jnp.exp(-jnp.abs(raw)))
    decay = step * (-LOG2E * jnp.exp(dlog_ref[...]))
    at = lax.broadcasted_iota(jnp.int32, (SPAN, SPAN), 0)
    by = lax.broadcasted_iota(jnp.int32, (SPAN, SPAN), 1)
    tri = (at >= by).astype(F32)
    before = jnp.zeros((1, heads), F32)
    last = jnp.zeros((1, heads), F32)
    for s in range(spans):
        at_rows = pl.ds(s * SPAN, SPAN)
        piece = decay[s * SPAN : (s + 1) * SPAN]
        cum = jnp.dot(tri, piece, precision=lax.Precision.HIGHEST, preferred_element_type=F32)
        total = cum[SPAN - 1 : SPAN]
        own = step[s * SPAN : (s + 1) * SPAN]
        dt_ref[at_rows, :heads] = own
        wst_ref[at_rows, :heads] = own * jnp.exp2(total - cum)
        cum_ref[at_rows, :heads] = cum
        ecum_ref[at_rows, :heads] = jnp.exp2(cum)
        edev_ref[at_rows, :heads] = jnp.exp2(cum + before)
        before = before + total
        last = total
    cumt_ref[...] = jnp.transpose(cum_ref[...])
    tot_ref[...] = before
    last_ref[...] = jnp.exp2(last)


def rates(step_input, step_offset, decay_log):
    rows, heads = step_input.shape
    wide = jax.ShapeDtypeStruct((rows, LANES), F32)
    row = jax.ShapeDtypeStruct((1, heads), F32)
    return pl.pallas_call(
        rates_kernel,
        out_shape=(wide, wide, wide, jax.ShapeDtypeStruct((LANES, rows), F32), wide, wide, row, row),
        in_specs=whole_vmem(3),
        out_specs=whole_vmem(8),
        cost_estimate=cost(1e9, 2e6),
        name="rates",
    )(step_input, step_offset[None, :], decay_log[None, :])


def filtered(source, taps, offset, length):
    total = offset
    for k in range(taps.shape[0]):
        total = total + taps[k : k + 1] * source(k, length)
    return (total + total * jnp.tanh(total)).astype(BF16)


def selector_kernel(sel_ref, tail_ref, taps_ref, off_ref, write_ref, read_ref, scores_ref, buf_ref):
    rows, width = sel_ref.shape
    count = tail_ref.shape[0]
    size = width // 2
    buf_ref[8 - count : 8, :] = tail_ref[...].astype(F32)
    buf_ref[8 : 8 + rows, :] = sel_ref[...].astype(F32)
    out = filtered(
        lambda k, length: buf_ref[8 - count + k : 8 - count + k + length, :],
        0.5 * taps_ref[...], 0.5 * off_ref[...], rows)
    write_ref[...] = jnp.transpose(out[:, :size].astype(F32)).astype(BF16)
    read_ref[...] = out[:, size:]
    at = lax.broadcasted_iota(jnp.int32, (SPAN, SPAN), 0)
    by = lax.broadcasted_iota(jnp.int32, (SPAN, SPAN), 1)
    for s in range(rows // SPAN):
        at_rows = pl.ds(s * SPAN, SPAN)
        got = dot(read_ref[at_rows, :], write_ref[:, s * SPAN : (s + 1) * SPAN])
        scores_ref[at_rows, :] = jnp.where(at >= by, got, 0.0)


def selectors(selector, tail, taps, offset):
    rows, width = selector.shape
    return pl.pallas_call(
        selector_kernel,
        out_shape=(
            jax.ShapeDtypeStruct((width // 2, rows), BF16),
            jax.ShapeDtypeStruct((rows, width // 2), BF16),
            jax.ShapeDtypeStruct((rows, SPAN), F32),
        ),
        in_specs=whole_vmem(4),
        out_specs=whole_vmem(3),
        scratch_shapes=[pltpu.VMEM((rows + 8, width), F32)],
        cost_estimate=cost(1e8, 2e6),
        name="selectors",
    )(selector, tail, taps, offset[None, :])


def states_kernel(group, start_ref, last_ref, x_ref, tail_ref, taps_ref, off_ref, wst_ref, write_ref,
                  conv_ref, local_ref, first_ref, buf_ref, weighted_ref):
    rows = x_ref.shape[0]
    count = tail_ref.shape[0]
    tile = 64
    head0 = (start_ref[0] + pl.program_id(0)) * group
    factors = pltpu.roll(wst_ref[...], LANES - head0, 1)
    for h in range(group):
        cols = slice(h * LANES, (h + 1) * LANES)
        buf_ref[h, 8 - count : 8, :] = tail_ref[:, cols].astype(F32)
        buf_ref[h, 8 : 8 + rows, :] = x_ref[:, cols].astype(F32)
        taps = 0.5 * taps_ref[:, cols]
        offset = 0.5 * off_ref[:, cols]
        for r in range(0, rows, tile):
            conv = filtered(
                lambda k, length: buf_ref[h, 8 - count + k + r : 8 - count + k + r + length, :],
                taps, offset, tile)
            conv_ref[r : r + tile, cols] = conv
            weighted_ref[r : r + tile, cols] = (
                factors[r : r + tile, h : h + 1] * conv.astype(F32)).astype(BF16)
    spans = rows // SPAN
    for h in range(0, group, 2):
        cols = slice(h * LANES, (h + 2) * LANES)
        got = [dot(write_ref[:, s * SPAN : (s + 1) * SPAN], weighted_ref[s * SPAN : (s + 1) * SPAN, cols])
               for s in range(spans)]
        for j in range(2):
            at_rows = slice((h + j) * LANES, (h + j + 1) * LANES)
            half = slice(j * LANES, (j + 1) * LANES)
            first = got[0][:, half]
            first_ref[at_rows, :] = first.astype(BF16)
            local_ref[at_rows, :] = (got[1][:, half] + last_ref[0, head0 + h + j] * first).astype(BF16)


def states(start, last, features, tail, taps, offset, wst, write, heads, group):
    rows = features.shape[0]
    count = tail.shape[0]
    steps = heads // group
    width = group * LANES
    spec = pltpu.PrefetchScalarGridSpec(
        num_scalar_prefetch=1,
        grid=(steps,),
        in_specs=[
            pl.BlockSpec(memory_space=SMEM),
            pl.BlockSpec((rows, width), lambda i, s: (0, s[0] + i)),
            pl.BlockSpec((count, width), lambda i, s: (0, s[0] + i)),
            pl.BlockSpec((taps.shape[0], width), lambda i, s: (0, s[0] + i)),
            pl.BlockSpec((1, width), lambda i, s: (0, s[0] + i)),
            pl.BlockSpec((rows, LANES), lambda i, s: (0, 0)),
            pl.BlockSpec(write.shape, lambda i, s: (0, 0)),
        ],
        out_specs=[
            pl.BlockSpec((rows, width), lambda i, s: (0, i)),
            pl.BlockSpec((width, LANES), lambda i, s: (i, 0)),
            pl.BlockSpec((width, LANES), lambda i, s: (i, 0)),
        ],
        scratch_shapes=[pltpu.VMEM((group, rows + 8, LANES), F32), pltpu.VMEM((rows, width), BF16)],
    )
    size = heads * LANES
    return pl.pallas_call(
        functools.partial(states_kernel, group),
        out_shape=(
            jax.ShapeDtypeStruct((rows, size), BF16),
            jax.ShapeDtypeStruct((size, LANES), BF16),
            jax.ShapeDtypeStruct((size, LANES), BF16),
        ),
        grid_spec=spec,
        cost_estimate=cost(heads * 20e6, 4 * rows * size),
        name="states",
    )(start, last, features, tail, taps, offset[None, :], wst, write)


def inner_kernel(group, start_ref, skip_ref, conv_ref, first_ref, dt_ref, cum_ref, ecum_ref, cumt_ref, scores_ref, read_ref, out_ref):
    rows = conv_ref.shape[0]
    half = SPAN // 2
    head0 = (start_ref[0] + pl.program_id(0)) * group
    shift = LANES - head0
    steps = pltpu.roll(dt_ref[...], shift, 1)
    cums = pltpu.roll(cum_ref[...], shift, 1)
    ecums = pltpu.roll(ecum_ref[...], shift, 1)
    for h in range(group):
        cols = slice(h * LANES, (h + 1) * LANES)
        row = cumt_ref[pl.ds(head0 + h, 1), :]
        skip = skip_ref[head0 + h]
        for s in range(rows // SPAN):
            top = slice(s * SPAN, s * SPAN + half)
            low = slice(s * SPAN + half, (s + 1) * SPAN)
            head_view = conv_ref[s * SPAN : (s + 1) * SPAN, cols].astype(F32)
            inputs = (steps[s * SPAN : (s + 1) * SPAN, h : h + 1] * head_view).astype(BF16)
            c_top, c_low = cums[top, h : h + 1], cums[low, h : h + 1]
            r_top, r_low = row[:, top], row[:, low]
            m00 = scores_ref[top, :half] * jnp.exp2(jnp.minimum(c_top - r_top, 0.0))
            m10 = scores_ref[low, :half] * jnp.exp2(c_low - r_top)
            m11 = scores_ref[low, half:] * jnp.exp2(jnp.minimum(c_low - r_low, 0.0))
            bottom = jnp.concatenate([m10.astype(BF16), m11.astype(BF16)], axis=1)
            y_top = dot(m00.astype(BF16), inputs[:half])
            y_low = dot(bottom, inputs)
            if s > 0:
                carried = dot(read_ref[s * SPAN : (s + 1) * SPAN, :], first_ref[cols, :])
                y_top = y_top + ecums[top, h : h + 1] * carried[:half]
                y_low = y_low + ecums[low, h : h + 1] * carried[half:]
            out_ref[top, cols] = (y_top + skip * head_view[:half]).astype(BF16)
            out_ref[low, cols] = (y_low + skip * head_view[half:]).astype(BF16)


def inner(start, skip, conv, first, dt, cum, ecum, cumt, scores, read, group):
    rows, size = conv.shape
    width = group * LANES
    fixed = lambda a: pl.BlockSpec(a.shape, lambda i, s: (0, 0))
    spec = pltpu.PrefetchScalarGridSpec(
        num_scalar_prefetch=1,
        grid=(size // width,),
        in_specs=[
            pl.BlockSpec(memory_space=SMEM),
            pl.BlockSpec((rows, width), lambda i, s: (0, i)),
            pl.BlockSpec((width, LANES), lambda i, s: (i, 0)),
            fixed(dt), fixed(cum), fixed(ecum), fixed(cumt), fixed(scores), fixed(read),
        ],
        out_specs=pl.BlockSpec((rows, width), lambda i, s: (0, i)),
    )
    return pl.pallas_call(
        functools.partial(inner_kernel, group),
        out_shape=jax.ShapeDtypeStruct((rows, size), BF16),
        grid_spec=spec,
        cost_estimate=cost(size // LANES * 50e6, 4 * rows * size),
        name="inner",
    )(start, skip, conv, first, dt, cum, ecum, cumt, scores, read)


def splat(value):
    return jnp.exp2(jnp.full((1, LANES), value, F32))


def pair_kernel(base, ids_ref, logs_ref, own_ref, got_ref, out_ref):
    side, pair = ids_ref[0], ids_ref[1]
    heads = own_ref.shape[0] // LANES
    head0 = base + side * heads

    def one(h, _):
        at_rows = pl.ds(pl.multiple_of(h * LANES, LANES), LANES)
        other = logs_ref[2 * pair + 1 - side, head0 + h]
        grown = splat(other)
        own, got = own_ref[at_rows, :].astype(F32), got_ref[at_rows, :].astype(F32)
        first = jnp.where(side == 0, own, got)
        second = jnp.where(side == 0, got, own)
        later = splat(logs_ref[2 * pair + 1, head0 + h])
        out_ref[at_rows, :] = (later * first + second).astype(BF16)
        return 0

    lax.fori_loop(0, heads, one, 0)


def pair_total(base, ids, logs, own, got):
    return pl.pallas_call(
        functools.partial(pair_kernel, base),
        out_shape=jax.ShapeDtypeStruct(own.shape, BF16),
        in_specs=[pl.BlockSpec(memory_space=SMEM)] * 2 + whole_vmem(2),
        out_specs=pl.BlockSpec(memory_space=VMEM),
        cost_estimate=cost(1e6, own.size * 6),
        name="pair_total",
    )(ids, logs, own, got)


def prefix_kernel(base, half, ids_ref, logs_ref, in_ref, out_ref):
    side, pair = ids_ref[0], ids_ref[1]
    pairs, rows, _ = in_ref.shape
    part = min(rows, LANES)
    for r in range(0, rows, part):
        head = base + side * half + (pair * rows + r) // LANES
        running = jnp.zeros((part, LANES), F32)
        for j in range(pairs):
            out_ref[j, r : r + part, :] = running.astype(BF16)
            grown = splat(logs_ref[2 * j, head] + logs_ref[2 * j + 1, head])
            running = grown * running + in_ref[j, r : r + part, :].astype(F32)


def prefix(base, half, ids, logs, totals):
    return pl.pallas_call(
        functools.partial(prefix_kernel, base, half),
        out_shape=jax.ShapeDtypeStruct(totals.shape, BF16),
        in_specs=[pl.BlockSpec(memory_space=SMEM)] * 2 + whole_vmem(1),
        out_specs=pl.BlockSpec(memory_space=VMEM),
        cost_estimate=cost(1e6, totals.size * 4),
        name="prefix",
    )(ids, logs, totals)


def split_kernel(base, ids_ref, logs_ref, in_ref, own_ref, got_ref, keep_ref, send_ref):
    side, pair = ids_ref[0], ids_ref[1]
    heads = own_ref.shape[0] // LANES
    head0 = base + side * heads

    def one(h, _):
        at_rows = pl.ds(pl.multiple_of(h * LANES, LANES), LANES)
        entering = in_ref[at_rows, :].astype(F32)
        first = jnp.where(side == 0, own_ref[at_rows, :].astype(F32), got_ref[at_rows, :].astype(F32))
        later = splat(logs_ref[2 * pair, head0 + h]) * entering + first
        keep_ref[at_rows, :] = jnp.where(side == 0, entering, later).astype(BF16)
        send_ref[at_rows, :] = jnp.where(side == 0, later, entering).astype(BF16)
        return 0

    lax.fori_loop(0, heads, one, 0)


def split_entering(base, ids, logs, entering, own, got):
    shape = jax.ShapeDtypeStruct(own.shape, BF16)
    return pl.pallas_call(
        functools.partial(split_kernel, base),
        out_shape=(shape, shape),
        in_specs=[pl.BlockSpec(memory_space=SMEM)] * 2 + whole_vmem(3),
        out_specs=whole_vmem(2),
        cost_estimate=cost(1e6, own.size * 10),
        name="split_entering",
    )(ids, logs, entering, own, got)


def finish_kernel(pieces, half, ids_ref, *refs):
    inner_refs, state_refs = refs[:pieces], refs[pieces : 2 * pieces]
    edev_ref, read_ref, gain_ref, out_ref, mixed_ref = refs[2 * pieces :]
    side = ids_ref[0]
    rows = read_ref.shape[0]
    width = half * LANES
    read = read_ref[...]
    square = jnp.zeros((rows, LANES), F32)
    for k in range(pieces):
        head0 = (k // 2) * 2 * half + (side if k % 2 == 0 else 1 - side) * half
        grown = pltpu.roll(edev_ref[...], LANES - head0, 1)
        for h in range(0, half, 2):
            state = jnp.concatenate(
                [state_refs[k][(h + j) * LANES : (h + j + 1) * LANES, :] for j in range(2)], axis=1)
            carried = dot(read, state)
            for j in range(2):
                cols = slice((h + j) * LANES, (h + j + 1) * LANES)
                value = (inner_refs[k][:, cols].astype(F32)
                         + grown[:, h + j : h + j + 1] * carried[:, j * LANES : (j + 1) * LANES])
                value = value.astype(BF16)
                mixed_ref[:, k * width + (h + j) * LANES : k * width + (h + j + 1) * LANES] = value
                value = value.astype(F32)
                square = square + value * value
    mean = jnp.sum(square, axis=1, keepdims=True) * (1.0 / (pieces * width))
    scale = lax.rsqrt(mean + 1e-05)
    for k in range(pieces):
        head0 = (k // 2) * 2 * half + (side if k % 2 == 0 else 1 - side) * half
        col0 = pl.multiple_of(head0 * LANES, LANES)
        for h in range(half):
            value = mixed_ref[:, k * width + h * LANES : k * width + (h + 1) * LANES].astype(F32)
            cols = pl.ds(pl.multiple_of(col0 + h * LANES, LANES), LANES)
            out_ref[:, cols] = (value * scale * gain_ref[:, cols]).astype(BF16)


def finish(ids, inners, entering, edev, read, gain, half):
    rows = read.shape[0]
    pieces = len(inners)
    width = half * LANES
    tile = 64
    spec = pltpu.PrefetchScalarGridSpec(
        num_scalar_prefetch=1,
        grid=(rows // tile,),
        in_specs=[pl.BlockSpec((tile, width), lambda i, s: (i, 0))] * pieces
        + [pl.BlockSpec((width, LANES), lambda i, s: (0, 0))] * pieces
        + [
            pl.BlockSpec((tile, LANES), lambda i, s: (i, 0)),
            pl.BlockSpec((tile, read.shape[1]), lambda i, s: (i, 0)),
            pl.BlockSpec((1, gain.shape[0]), lambda i, s: (0, 0)),
        ],
        out_specs=pl.BlockSpec((tile, gain.shape[0]), lambda i, s: (i, 0)),
        scratch_shapes=[pltpu.VMEM((tile, gain.shape[0]), BF16)],
    )
    return pl.pallas_call(
        functools.partial(finish_kernel, pieces, half),
        out_shape=jax.ShapeDtypeStruct((rows, gain.shape[0]), BF16),
        grid_spec=spec,
        cost_estimate=cost(2e9, 4 * rows * gain.shape[0]),
        name="finish",
    )(ids, *inners, *entering, edev, read, gain[None, :])


def exchanged(block):
    return lax.ppermute(block, "side", [(0, 1), (1, 0)])


def scattered(block, peers):
    return lax.all_to_all(block.reshape(peers, -1, LANES), GROUP, 0, 0)


def on_device(
    features,
    selector,
    step_input,
    feature_kernel,
    selector_kernel,
    feature_offset,
    selector_offset,
    decay_log,
    step_offset,
    skip_scale,
    norm_gain,
):
    rows, channels = features.shape
    heads = decay_log.shape[0]
    tail_count = feature_kernel.shape[0] - 1
    devices = lax.axis_size(ALL)
    peers = lax.axis_size(GROUP)
    side = lax.axis_index("side")
    pair = lax.axis_index(GROUP)
    ids = jnp.stack([side, pair]).astype(jnp.int32)
    chunks = 3
    half = heads // (2 * chunks)
    group = 4

    last_rows = jnp.concatenate([features[rows - tail_count :], selector[rows - tail_count :]], axis=1)
    tail = lax.ppermute(last_rows, ALL, [(i, i + 1) for i in range(devices - 1)])
    dt, wst, cum, cumt, ecum, edev, total, last = rates(step_input, step_offset, decay_log)
    logs = lax.all_to_all(jnp.broadcast_to(total, (devices, heads)), ALL, 0, 0, tiled=True)
    write, read, scores = selectors(selector, tail[:, channels:], selector_kernel, selector_offset)

    convs, firsts, locals_, starts = [], [], [], []
    for c in range(chunks):
        for other in (True, False):
            which = (1 - side) if other else side
            start = ((2 * c + which) * (half // group)).astype(jnp.int32)[None]
            conv, local, first = states(
                start, last, features, tail, feature_kernel, feature_offset, wst, write, half, group)
            convs.append(conv)
            locals_.append(local)
            firsts.append(first)
            starts.append(start)
    inners = [
        inner(starts[k], skip_scale, convs[k], firsts[k], dt, cum, ecum, cumt, scores, read, group)
        for k in range(2 * chunks)
    ]
    pieces, entering = [], []
    for c in range(chunks):
        base = 2 * half * c
        theirs, own = locals_[2 * c], locals_[2 * c + 1]
        got = exchanged(theirs)
        totals = scattered(pair_total(base, ids, logs, own, got), peers)
        entered = scattered(prefix(base, half, ids, logs, totals), peers)
        keep, send = split_entering(base, ids, logs, entered.reshape(own.shape), own, got)
        pieces += [inners[2 * c + 1], inners[2 * c]]
        entering += [keep, exchanged(send)]
    return finish(ids, pieces, entering, edev, read, norm_gain, half)


def solution(mesh):
    devices = mesh.devices
    fine = Mesh(devices.reshape(devices.shape[0], devices.shape[1] // 2, 2), ALL)
    rows = P(ALL, None)
    return jax.shard_map(
        on_device, mesh=fine, in_specs=(rows,) * 3 + (P(),) * 8, out_specs=rows, check_vma=False
    )
```

time: 1050 us -> 255 us (0.24)
  blocking collectives: 285 us -> 0 us
  waiting for transfers between devices: 305 us -> 63.3 us
  local copies, waits for them, and re-layouts: 204 us -> 8.92 us
  other arithmetic: 185 us -> 0.71 us
  Pallas kernels: 0 us -> 134 us
  matrix products: 32.8 us -> 0 us
  starting transfers between devices: 17 us -> 44.9 us
  between operations: 14.4 us -> 0.22 us
    all_to_all x1 -> x0, blocking collectives: 280 us -> none  [on_device(): lax.all_to_all(mixed, 'head', split_axis=0, concat_axis=1, tiled=True)]
    all_gather x2 -> x0, waiting for transfers between devices: 249 us -> none  [the longest x1 238 us: on_device(): selector_slab = lax.all_gather(selector_send, 'head', axis=0, tiled=True)]
    pallas_call x0 -> x24, Pallas kernels: none -> 134 us  [the longest x6 41.8 us: inner(): pl.pallas_call(functools.partial(inner_kernel, group), out_shape=jax.Shap...]
    convert_element_type x12 -> x0, other arithmetic: 130 us -> none  [the longest x2 60.5 us: causal_filter(): return jax.nn.silu(summed).astype(jnp.bfloat16)]
    dynamic_update_slice x12 -> x0, local copies, waits for them, and re-layouts: 56.4 us -> none  [the longest x4 29.4 us: selective_rows(): lax.map(run_output, (diagonal, cumulative, read_groups, regroup_entering,...]
    convert_element_type x4 -> x0, local copies, waits for them, and re-layouts: 41.5 us -> none  [the longest x1 24.7 us: normalize(): widened = values.astype(jnp.float32)]
    dynamic_slice x12 -> x0, local copies, waits for them, and re-layouts: 39.9 us -> none  [the longest x4 26.8 us: selective_rows(): lax.map(run_output, (diagonal, cumulative, read_groups, regroup_entering,...]
    dot_general x6 -> x0, matrix products: 29.2 us -> none  [the longest x2 19.4 us: span_terms(): jnp.einsum('hij,jhp->ihp', mixing, inputs, preferred_element_type=jnp.flo...]
  transfers between devices with their start and end apart: 5 -> 14, of which waited for: 3 -> 7; matrix products, arithmetic and copies ran while one was open for 10% -> 1% of each run, Pallas kernels for 0% -> 38%
where the time goes in v1:
time: 255 us; the launch traced here: 253 us
  Pallas kernels  134 us (53%)
  waiting for transfers between devices  63.3 us (25%)
  starting transfers between devices  44.9 us (18%)
  local copies, waits for them, and re-layouts  8.92 us (3%)
    all_to_all x6, waiting for transfers between devices, scattered(): return lax.all_to_all(block.reshape(peers, -1, LANES), GROUP, 0, 0)  48.4 us
    pallas_call x6, Pallas kernels, inner(): pl.pallas_call(functools.partial(inner_kernel, group), out_shape=jax.Shap...  41.8 us
    pallas_call x6, Pallas kernels, states(): pl.pallas_call(functools.partial(states_kernel, group), out_shape=(jax.Sh...  37.1 us
    pallas_call x1, Pallas kernels, finish(): pl.pallas_call(functools.partial(finish_kernel, pieces, half), out_shape=...  28.8 us
    all_to_all x6, starting transfers between devices, scattered(): return lax.all_to_all(block.reshape(peers, -1, LANES), GROUP, 0, 0)  26.9 us
    ppermute x6, waiting for transfers between devices, exchanged(): return lax.ppermute(block, 'side', [(0, 1), (1, 0)])  13.6 us
    pallas_call x3, Pallas kernels, split_entering(): pl.pallas_call(functools.partial(split_kernel, base), out_shape=(shape, s...  8.33 us
    ppermute x6, starting transfers between devices, exchanged(): return lax.ppermute(block, 'side', [(0, 1), (1, 0)])  8.21 us
  transfers between devices with their start and end apart: 14, of which 7 were waited for; matrix products, arithmetic and copies ran while one was open for 1% of the time, Pallas kernels for 38%

profile of v1, /device:TPU:0, one launch (start us, length us, event | category | flops | bytes accessed | tf_op | source)
XLA Modules:
  0.0 252.5 jit_solution(13186816608845525762)
XLA Ops:
  1.7 4.9 %collective-permute-start = (bf16[3,12544]{1,0:T(4,128)(2,1)S(1)}, bf16[3,12544]{1,0:T(4,128)(2,1)S(1)}, u32[]{:S(2)}, u32[]{:S(2)}) collective-permute-start(bf16[3,12544]{1,0:T(4,128)(2,1)S(1)} %pad_maximum_fusion), channel_id=1, source_target_pairs={{0,1},{1,2},{2,3},{3,4},{4,5},{5,6},{6,7},{7,8},{8,9},{9,10},{10,1... | collective-permute-start | bytes 225800 | tf_op jit(solution)/shard_map/ppermute | solution.py:431
  8.3 2.9 %rates.1 = (f32[512,128]{1,0:T(8,128)}, f32[512,128]{1,0:T(8,128)}, f32[512,128]{1,0:T(8,128)}, f32[128,512]{1,0:T(8,128)}, f32[512,128]{1,0:T(8,128)}, /*index=...) custom-call(bf16[512,96]{1,0:T(8,128)(2,1)} %copy.13.step_ref, f32[1,96]{1,0:T(1,128)} %bitcast.45, f32[1,96]{1,0:T(1,128)} %bitcast.46), custom_call_target="tpu_custom_call" | custom-call | flops 1000000000 | bytes 2000000 | tf_op jit(solution)/shard_map/rates/pallas_call | solution.py:68
  11.8 2.4 selectors.1
  14.2 6.2 %states.11 = (bf16[512,2048]{1,0:T(8,128)(2,1)}, bf16[2048,128]{1,0:T(8,128)(2,1)}, bf16[2048,128]{1,0:T(8,128)(2,1)}) custom-call(s32[1]{0:T(128)} %bitcast.11.start_ref, f32[1,96]{1,0:T(1,128)} %get-tuple-element.40.last_ref, bf16[512,12288]{1,0:T(8,128)(2,1)} %x_ref.11, bf16[3,12544]{1,0:T(4,128)(2,1)} %copy-done, f32[4,12288]{1,0:T(4,128)} %taps_ref.13, ...), custom_call_target="tpu_custom_call" | custom-call | flops 320000000 | bytes 4194304 | tf_op jit(solution)/shard_map/states/pallas_call | solution.py:179
  22.6 4.8 %all-to-all-start = ((f32[32,1,96]{2,1,0:T(1,128)}), f32[32,1,96]{2,1,0:T(1,128)S(1)}, u32[]{:S(2)}, u32[]{:S(2)}) async-start(f32[32,1,96]{2,1,0:T(1,128)} %broadcast_in_dim.53), calls=%async_computation | async-start | bytes 32768 | tf_op jit(solution)/shard_map/all_to_all | solution.py:433
  28.1 6.2 %states.10 = (bf16[512,2048]{1,0:T(8,128)(2,1)}, bf16[2048,128]{1,0:T(8,128)(2,1)}, bf16[2048,128]{1,0:T(8,128)(2,1)}) custom-call(s32[1]{0:T(128)} %bitcast.10.start_ref, f32[1,96]{1,0:T(1,128)} %get-tuple-element.40.last_ref, bf16[512,12288]{1,0:T(8,128)(2,1)} %x_ref.11, bf16[3,12544]{1,0:T(4,128)(2,1)} %copy-done, f32[4,12288]{1,0:T(4,128)} %taps_ref.13, ...), custom_call_target="tpu_custom_call" | custom-call | flops 320000000 | bytes 4194304 | tf_op jit(solution)/shard_map/states/pallas_call | solution.py:179
  38.8 4.6 %all-to-all-start.5 = ((bf16[16,128,128]{2,1,0:T(8,128)(2,1)}), bf16[16,128,128]{2,1,0:T(8,128)(2,1)S(1)}, u32[]{:S(2)}, u32[]{:S(2)}) async-start(bf16[16,128,128]{2,1,0:T(8,128)(2,1)} %bitcast.25), calls=%async_computation.5 | async-start | bytes 1048576 | tf_op jit(solution)/shard_map/all_to_all | solution.py:402
  43.4 6.2 %states.9 = (bf16[512,2048]{1,0:T(8,128)(2,1)}, bf16[2048,128]{1,0:T(8,128)(2,1)}, bf16[2048,128]{1,0:T(8,128)(2,1)}) custom-call(s32[1]{0:T(128)} %bitcast.9.start_ref, f32[1,96]{1,0:T(1,128)} %get-tuple-element.40.last_ref, bf16[512,12288]{1,0:T(8,128)(2,1)} %x_ref.11, bf16[3,12544]{1,0:T(4,128)(2,1)} %copy-done, f32[4,12288]{1,0:T(4,128)} %taps_ref.13, ...), custom_call_target="tpu_custom_call" | custom-call | flops 320000000 | bytes 4194304 | tf_op jit(solution)/shard_map/states/pallas_call | solution.py:179
  51.2 6.2 %states.8 = (bf16[512,2048]{1,0:T(8,128)(2,1)}, bf16[2048,128]{1,0:T(8,128)(2,1)}, bf16[2048,128]{1,0:T(8,128)(2,1)}) custom-call(s32[1]{0:T(128)} %bitcast.8.start_ref, f32[1,96]{1,0:T(1,128)} %get-tuple-element.40.last_ref, bf16[512,12288]{1,0:T(8,128)(2,1)} %x_ref.11, bf16[3,12544]{1,0:T(4,128)(2,1)} %copy-done, f32[4,12288]{1,0:T(4,128)} %taps_ref.13, ...), custom_call_target="tpu_custom_call" | custom-call | flops 320000000 | bytes 4194304 | tf_op jit(solution)/shard_map/states/pallas_call | solution.py:179
  57.4 6.7 %collective-permute-done.3.got_ref = bf16[2048,128]{1,0:T(8,128)(2,1)S(1)} collective-permute-done((bf16[2048,128]{1,0:T(8,128)(2,1)}, bf16[2048,128]{1,0:T(8,128)(2,1)S(1)}, u32[]{:S(2)}, u32[]{:S(2)}) %collective-permute-start.3) | collective-permute-done | bytes 524320 | tf_op jit(solution)/shard_map/ppermute | solution.py:398
  67.3 5.7 %all-to-all-start.3 = ((bf16[16,128,128]{2,1,0:T(8,128)(2,1)}), bf16[16,128,128]{2,1,0:T(8,128)(2,1)S(1)}, u32[]{:S(2)}, u32[]{:S(2)}) async-start(bf16[16,128,128]{2,1,0:T(8,128)(2,1)} %bitcast.21), calls=%async_computation.3 | async-start | bytes 1048576 | tf_op jit(solution)/shard_map/all_to_all | solution.py:402
  73.0 6.2 %states.7 = (bf16[512,2048]{1,0:T(8,128)(2,1)}, bf16[2048,128]{1,0:T(8,128)(2,1)}, bf16[2048,128]{1,0:T(8,128)(2,1)}) custom-call(s32[1]{0:T(128)} %bitcast.7.start_ref, f32[1,96]{1,0:T(1,128)} %get-tuple-element.40.last_ref, bf16[512,12288]{1,0:T(8,128)(2,1)} %x_ref.11, bf16[3,12544]{1,0:T(4,128)(2,1)} %copy-done, f32[4,12288]{1,0:T(4,128)} %taps_ref.13, ...), custom_call_target="tpu_custom_call" | custom-call | flops 320000000 | bytes 4194304 | tf_op jit(solution)/shard_map/states/pallas_call | solution.py:179
  80.8 6.1 %states.6 = (bf16[512,2048]{1,0:T(8,128)(2,1)}, bf16[2048,128]{1,0:T(8,128)(2,1)}, bf16[2048,128]{1,0:T(8,128)(2,1)}) custom-call(s32[1]{0:T(128)} %bitcast.2.start_ref, f32[1,96]{1,0:T(1,128)} %get-tuple-element.40.last_ref, bf16[512,12288]{1,0:T(8,128)(2,1)} %x_ref.11, bf16[3,12544]{1,0:T(4,128)(2,1)} %copy-done, f32[4,12288]{1,0:T(4,128)} %taps_ref.13, ...), custom_call_target="tpu_custom_call" | custom-call | flops 320000000 | bytes 4194304 | tf_op jit(solution)/shard_map/states/pallas_call | solution.py:179
  87.0 6.8 %collective-permute-done.1.got_ref = bf16[2048,128]{1,0:T(8,128)(2,1)S(1)} collective-permute-done((bf16[2048,128]{1,0:T(8,128)(2,1)}, bf16[2048,128]{1,0:T(8,128)(2,1)S(1)}, u32[]{:S(2)}, u32[]{:S(2)}) %collective-permute-start.1) | collective-permute-done | bytes 524320 | tf_op jit(solution)/shard_map/ppermute | solution.py:398
  97.0 5.7 %all-to-all-start.1 = ((bf16[16,128,128]{2,1,0:T(8,128)(2,1)}), bf16[16,128,128]{2,1,0:T(8,128)(2,1)S(1)}, u32[]{:S(2)}, u32[]{:S(2)}) async-start(bf16[16,128,128]{2,1,0:T(8,128)(2,1)} %bitcast.26), calls=%async_computation.1 | async-start | bytes 1048576 | tf_op jit(solution)/shard_map/all_to_all | solution.py:402
  104.7 13.6 %all-to-all-done.1.in_ref = bf16[16,128,128]{2,1,0:T(8,128)(2,1)S(1)} async-done(((bf16[16,128,128]{2,1,0:T(8,128)(2,1)}), bf16[16,128,128]{2,1,0:T(8,128)(2,1)S(1)}, u32[]{:S(2)}, u32[]{:S(2)}) %all-to-all-start.1) | async-done | bytes 524320 | tf_op jit(solution)/shard_map/all_to_all | solution.py:402
  118.2 3.6 %all-to-all-start.6 = ((bf16[16,128,128]{2,1,0:T(8,128)(2,1)}), bf16[16,128,128]{2,1,0:T(8,128)(2,1)S(1)}, u32[]{:S(2)}, u32[]{:S(2)}) async-start(bf16[16,128,128]{2,1,0:T(8,128)(2,1)} %prefix.5), calls=%async_computation.6 | async-start | bytes 1048576 | tf_op jit(solution)/shard_map/all_to_all | solution.py:402
  123.8 13.5 %all-to-all-done.6 = bf16[16,128,128]{2,1,0:T(8,128)(2,1)S(1)} async-done(((bf16[16,128,128]{2,1,0:T(8,128)(2,1)}), bf16[16,128,128]{2,1,0:T(8,128)(2,1)S(1)}, u32[]{:S(2)}, u32[]{:S(2)}) %all-to-all-start.6) | async-done | bytes 524320 | tf_op jit(solution)/shard_map/all_to_all | solution.py:402
  137.4 3.6 %all-to-all-start.4 = ((bf16[16,128,128]{2,1,0:T(8,128)(2,1)}), bf16[16,128,128]{2,1,0:T(8,128)(2,1)S(1)}, u32[]{:S(2)}, u32[]{:S(2)}) async-start(bf16[16,128,128]{2,1,0:T(8,128)(2,1)} %prefix.4), calls=%async_computation.4 | async-start | bytes 1048576 | tf_op jit(solution)/shard_map/all_to_all | solution.py:402
  142.9 13.5 %all-to-all-done.4 = bf16[16,128,128]{2,1,0:T(8,128)(2,1)S(1)} async-done(((bf16[16,128,128]{2,1,0:T(8,128)(2,1)}), bf16[16,128,128]{2,1,0:T(8,128)(2,1)S(1)}, u32[]{:S(2)}, u32[]{:S(2)}) %all-to-all-start.4) | async-done | bytes 524320 | tf_op jit(solution)/shard_map/all_to_all | solution.py:402
  156.5 3.8 %all-to-all-start.2 = ((bf16[16,128,128]{2,1,0:T(8,128)(2,1)}), bf16[16,128,128]{2,1,0:T(8,128)(2,1)S(1)}, u32[]{:S(2)}, u32[]{:S(2)}) async-start(bf16[16,128,128]{2,1,0:T(8,128)(2,1)} %prefix.3), calls=%async_computation.2 | async-start | bytes 1048576 | tf_op jit(solution)/shard_map/all_to_all | solution.py:402
  160.3 2.8 %split_entering.5 = (bf16[2048,128]{1,0:T(8,128)(2,1)}, bf16[2048,128]{1,0:T(8,128)(2,1)}) custom-call(s32[2]{0:T(128)} %pad_add_fusion.ids_ref, f32[32,96]{1,0:T(8,128)} %bitcast.39, bf16[2048,128]{1,0:T(8,128)(2,1)} %bitcast.23, bf16[2048,128]{1,0:T(8,128)(2,1)} %get-tuple-element.70.own_ref, bf16[2048,128]{1,0:T(8,128)(2,1)} %copy-done.1), custom_call_target="tpu_custom_call" | custom-call | flops 1000000 | bytes 2621440 | tf_op jit(solution)/shard_map/split_entering/pallas_call | solution.py:326
  164.5 2.8 %split_entering.4 = (bf16[2048,128]{1,0:T(8,128)(2,1)}, bf16[2048,128]{1,0:T(8,128)(2,1)}) custom-call(s32[2]{0:T(128)} %pad_add_fusion.ids_ref, f32[32,96]{1,0:T(8,128)} %bitcast.40, bf16[2048,128]{1,0:T(8,128)(2,1)} %bitcast.24, bf16[2048,128]{1,0:T(8,128)(2,1)} %get-tuple-element.66.own_ref, bf16[2048,128]{1,0:T(8,128)(2,1)} %copy-done.2), custom_call_target="tpu_custom_call" | custom-call | flops 1000000 | bytes 2621440 | tf_op jit(solution)/shard_map/split_entering/pallas_call | solution.py:326
  167.9 7.8 %all-to-all-done.2 = bf16[16,128,128]{2,1,0:T(8,128)(2,1)S(1)} async-done(((bf16[16,128,128]{2,1,0:T(8,128)(2,1)}), bf16[16,128,128]{2,1,0:T(8,128)(2,1)S(1)}, u32[]{:S(2)}, u32[]{:S(2)}) %all-to-all-start.2) | async-done | bytes 524320 | tf_op jit(solution)/shard_map/all_to_all | solution.py:402
  176.4 2.8 %split_entering.3 = (bf16[2048,128]{1,0:T(8,128)(2,1)}, bf16[2048,128]{1,0:T(8,128)(2,1)}) custom-call(s32[2]{0:T(128)} %pad_add_fusion.ids_ref, f32[32,96]{1,0:T(8,128)} %bitcast.41, bf16[2048,128]{1,0:T(8,128)(2,1)} %bitcast.22, bf16[2048,128]{1,0:T(8,128)(2,1)} %get-tuple-element.62.own_ref, bf16[2048,128]{1,0:T(8,128)(2,1)} %copy-done.3), custom_call_target="tpu_custom_call" | custom-call | flops 1000000 | bytes 2621440 | tf_op jit(solution)/shard_map/split_entering/pallas_call | solution.py:326
  180.7 6.9 %inner.11.refs_5_ = bf16[512,2048]{1,0:T(8,128)(2,1)} custom-call(s32[1]{0:T(128)} %bitcast.11.start_ref, f32[96]{0:T(128)} %skip_ref.11, bf16[512,2048]{1,0:T(8,128)(2,1)} %get-tuple-element.59.conv_ref, bf16[2048,128]{1,0:T(8,128)(2,1)} %get-tuple-element.60.first_ref, f32[512,128]{1,0:T(8,128)} %get-tuple-element.45.dt_ref, ...), custom_call_target="tpu_custom_call" | custom-call | flops 800000000 | bytes 4194304 | tf_op jit(solution)/shard_map/inner/pallas_call | solution.py:240
  187.6 7.0 %inner.10.refs_4_ = bf16[512,2048]{1,0:T(8,128)(2,1)} custom-call(s32[1]{0:T(128)} %bitcast.10.start_ref, f32[96]{0:T(128)} %skip_ref.11, bf16[512,2048]{1,0:T(8,128)(2,1)} %get-tuple-element.57.conv_ref, bf16[2048,128]{1,0:T(8,128)(2,1)} %get-tuple-element.58.first_ref, f32[512,128]{1,0:T(8,128)} %get-tuple-element.45.dt_ref, ...), custom_call_target="tpu_custom_call" | custom-call | flops 800000000 | bytes 4194304 | tf_op jit(solution)/shard_map/inner/pallas_call | solution.py:240
  194.6 7.0 %inner.9.refs_3_ = bf16[512,2048]{1,0:T(8,128)(2,1)} custom-call(s32[1]{0:T(128)} %bitcast.9.start_ref, f32[96]{0:T(128)} %skip_ref.11, bf16[512,2048]{1,0:T(8,128)(2,1)} %get-tuple-element.55.conv_ref, bf16[2048,128]{1,0:T(8,128)(2,1)} %get-tuple-element.56.first_ref, f32[512,128]{1,0:T(8,128)} %get-tuple-element.45.dt_ref, ...), custom_call_target="tpu_custom_call" | custom-call | flops 800000000 | bytes 4194304 | tf_op jit(solution)/shard_map/inner/pallas_call | solution.py:240
  201.6 7.0 %inner.8.refs_2_ = bf16[512,2048]{1,0:T(8,128)(2,1)} custom-call(s32[1]{0:T(128)} %bitcast.8.start_ref, f32[96]{0:T(128)} %skip_ref.11, bf16[512,2048]{1,0:T(8,128)(2,1)} %get-tuple-element.53.conv_ref, bf16[2048,128]{1,0:T(8,128)(2,1)} %get-tuple-element.54.first_ref, f32[512,128]{1,0:T(8,128)} %get-tuple-element.45.dt_ref, ...), custom_call_target="tpu_custom_call" | custom-call | flops 800000000 | bytes 4194304 | tf_op jit(solution)/shard_map/inner/pallas_call | solution.py:240
  208.6 7.0 %inner.7.refs_1_ = bf16[512,2048]{1,0:T(8,128)(2,1)} custom-call(s32[1]{0:T(128)} %bitcast.7.start_ref, f32[96]{0:T(128)} %skip_ref.11, bf16[512,2048]{1,0:T(8,128)(2,1)} %get-tuple-element.51.conv_ref, bf16[2048,128]{1,0:T(8,128)(2,1)} %get-tuple-element.52.first_ref, f32[512,128]{1,0:T(8,128)} %get-tuple-element.45.dt_ref, ...), custom_call_target="tpu_custom_call" | custom-call | flops 800000000 | bytes 4194304 | tf_op jit(solution)/shard_map/inner/pallas_call | solution.py:240
  215.5 7.0 %inner.6.refs_0_ = bf16[512,2048]{1,0:T(8,128)(2,1)} custom-call(s32[1]{0:T(128)} %bitcast.2.start_ref, f32[96]{0:T(128)} %skip_ref.11, bf16[512,2048]{1,0:T(8,128)(2,1)} %get-tuple-element.43.conv_ref, bf16[2048,128]{1,0:T(8,128)(2,1)} %get-tuple-element.44.first_ref, f32[512,128]{1,0:T(8,128)} %get-tuple-element.45.dt_ref, ...), custom_call_target="tpu_custom_call" | custom-call | flops 800000000 | bytes 4194304 | tf_op jit(solution)/shard_map/inner/pallas_call | solution.py:240
  223.7 28.8 %finish.1 = bf16[512,12288]{1,0:T(8,128)(2,1)} custom-call(s32[2]{0:T(128)} %pad_add_fusion.ids_ref, bf16[512,2048]{1,0:T(8,128)(2,1)} %inner.6.refs_0_, bf16[512,2048]{1,0:T(8,128)(2,1)} %inner.7.refs_1_, bf16[512,2048]{1,0:T(8,128)(2,1)} %inner.8.refs_2_, bf16[512,2048]{1,0:T(8,128)(2,1)} %inner.9.refs_3_, bf16[512,2048]{1,0:T(8,128)(2,1)} %inner.10.refs_4_, ...), custom_call_target="tpu_custom_call" | custom-call | flops 2000000000 | bytes 25165824 | tf_op jit(solution)/shard_map/finish/pallas_call | solution.py:388
  (57 shorter events, 32.3 us)
Async XLA Ops:
  1.7 9.5 %collective-permute-start = (bf16[3,12544]{1,0:T(4,128)(2,1)S(1)}, bf16[3,12544]{1,0:T(4,128)(2,1)S(1)}, u32[]{:S(2)}, u32[]{:S(2)}) collective-permute-start(bf16[3,12544]{1,0:T(4,128)(2,1)S(1)} %pad_maximum_fusion), channel_id=1, source_target_pairs={{0,1},{1,2},{2,3},{3,4},{4,5},{5,6},{6,7},{7,8},{8,9},{9,10},{10,1... | collective-permute-start | bytes 225800 | tf_op jit(solution)/shard_map/ppermute | solution.py:431
  11.2 3.0 %copy-start = (bf16[3,12544]{1,0:T(4,128)(2,1)}, bf16[3,12544]{1,0:T(4,128)(2,1)S(1)}, u32[]{:S(2)}) copy-start(bf16[3,12544]{1,0:T(4,128)(2,1)S(1)} %collective-permute-done.tail_ref) | copy-start | bytes 225796
  14.2 7.7 %copy-start.14 = (f32[1,96]{1,0:T(1,128)S(1)}, f32[1,96]{1,0:T(1,128)}, u32[]{:S(2)}) copy-start(f32[1,96]{1,0:T(1,128)} %get-tuple-element.61) | copy-start | bytes 1156
  20.4 15.2 %collective-permute-start.5 = (bf16[2048,128]{1,0:T(8,128)(2,1)}, bf16[2048,128]{1,0:T(8,128)(2,1)S(1)}, u32[]{:S(2)}, u32[]{:S(2)}) collective-permute-start(bf16[2048,128]{1,0:T(8,128)(2,1)} %get-tuple-element.71), channel_id=1, source_target_pairs={{0,1},{1,0},{2,3},{3,2},{4,5},{5,4},{6,7},{7,6},{8,9},{9,8},{10,11... | collective-permute-start | bytes 1572872 | tf_op jit(solution)/shard_map/ppermute | solution.py:398
  22.6 13.0 %all-to-all-start = ((f32[32,1,96]{2,1,0:T(1,128)}), f32[32,1,96]{2,1,0:T(1,128)S(1)}, u32[]{:S(2)}, u32[]{:S(2)}) async-start(f32[32,1,96]{2,1,0:T(1,128)} %broadcast_in_dim.53), calls=%async_computation | async-start | bytes 32768 | tf_op jit(solution)/shard_map/all_to_all | solution.py:433
  35.6 0.6 copy-start.10
  35.6 0.8 copy-start.1
  38.8 28.5 %all-to-all-start.5 = ((bf16[16,128,128]{2,1,0:T(8,128)(2,1)}), bf16[16,128,128]{2,1,0:T(8,128)(2,1)S(1)}, u32[]{:S(2)}, u32[]{:S(2)}) async-start(bf16[16,128,128]{2,1,0:T(8,128)(2,1)} %bitcast.25), calls=%async_computation.5 | async-start | bytes 1048576 | tf_op jit(solution)/shard_map/all_to_all | solution.py:402
  49.6 14.5 %collective-permute-start.3 = (bf16[2048,128]{1,0:T(8,128)(2,1)}, bf16[2048,128]{1,0:T(8,128)(2,1)S(1)}, u32[]{:S(2)}, u32[]{:S(2)}) collective-permute-start(bf16[2048,128]{1,0:T(8,128)(2,1)} %get-tuple-element.67), channel_id=1, source_target_pairs={{0,1},{1,0},{2,3},{3,2},{4,5},{5,4},{6,7},{7,6},{8,9},{9,8},{10,11... | collective-permute-start | bytes 1572872 | tf_op jit(solution)/shard_map/ppermute | solution.py:398
  64.1 0.8 copy-start.2
  67.3 12.0 %copy-start.4 = (bf16[16,128,128]{2,1,0:T(8,128)(2,1)}, bf16[16,128,128]{2,1,0:T(8,128)(2,1)S(1)}, u32[]{:S(2)}) copy-start(bf16[16,128,128]{2,1,0:T(8,128)(2,1)S(1)} %all-to-all-done.5.in_ref) | copy-start | bytes 1572868
  67.3 29.6 %all-to-all-start.3 = ((bf16[16,128,128]{2,1,0:T(8,128)(2,1)}), bf16[16,128,128]{2,1,0:T(8,128)(2,1)S(1)}, u32[]{:S(2)}, u32[]{:S(2)}) async-start(bf16[16,128,128]{2,1,0:T(8,128)(2,1)} %bitcast.21), calls=%async_computation.3 | async-start | bytes 1048576 | tf_op jit(solution)/shard_map/all_to_all | solution.py:402
  79.3 14.5 %collective-permute-start.1 = (bf16[2048,128]{1,0:T(8,128)(2,1)}, bf16[2048,128]{1,0:T(8,128)(2,1)S(1)}, u32[]{:S(2)}, u32[]{:S(2)}) collective-permute-start(bf16[2048,128]{1,0:T(8,128)(2,1)} %get-tuple-element.63), channel_id=1, source_target_pairs={{0,1},{1,0},{2,3},{3,2},{4,5},{5,4},{6,7},{7,6},{8,9},{9,8},{10,11... | collective-permute-start | bytes 1572872 | tf_op jit(solution)/shard_map/ppermute | solution.py:398
  93.8 0.8 copy-start.3
  97.0 24.9 %copy-start.5 = (bf16[16,128,128]{2,1,0:T(8,128)(2,1)}, bf16[16,128,128]{2,1,0:T(8,128)(2,1)S(1)}, u32[]{:S(2)}) copy-start(bf16[16,128,128]{2,1,0:T(8,128)(2,1)S(1)} %all-to-all-done.3.in_ref) | copy-start | bytes 1572868
  97.0 21.3 %all-to-all-start.1 = ((bf16[16,128,128]{2,1,0:T(8,128)(2,1)}), bf16[16,128,128]{2,1,0:T(8,128)(2,1)S(1)}, u32[]{:S(2)}, u32[]{:S(2)}) async-start(bf16[16,128,128]{2,1,0:T(8,128)(2,1)} %bitcast.26), calls=%async_computation.1 | async-start | bytes 1048576 | tf_op jit(solution)/shard_map/all_to_all | solution.py:402
  118.2 22.7 %copy-start.9 = (bf16[16,128,128]{2,1,0:T(8,128)(2,1)}, bf16[16,128,128]{2,1,0:T(8,128)(2,1)S(1)}, u32[]{:S(2)}) copy-start(bf16[16,128,128]{2,1,0:T(8,128)(2,1)S(1)} %all-to-all-done.1.in_ref) | copy-start | bytes 1572868
  118.2 19.1 %all-to-all-start.6 = ((bf16[16,128,128]{2,1,0:T(8,128)(2,1)}), bf16[16,128,128]{2,1,0:T(8,128)(2,1)S(1)}, u32[]{:S(2)}, u32[]{:S(2)}) async-start(bf16[16,128,128]{2,1,0:T(8,128)(2,1)} %prefix.5), calls=%async_computation.6 | async-start | bytes 1048576 | tf_op jit(solution)/shard_map/all_to_all | solution.py:402
  137.4 22.9 %copy-start.7 = (bf16[16,128,128]{2,1,0:T(8,128)(2,1)}, bf16[16,128,128]{2,1,0:T(8,128)(2,1)S(1)}, u32[]{:S(2)}) copy-start(bf16[16,128,128]{2,1,0:T(8,128)(2,1)S(1)} %all-to-all-done.6) | copy-start | bytes 1572868
  137.4 19.1 %all-to-all-start.4 = ((bf16[16,128,128]{2,1,0:T(8,128)(2,1)}), bf16[16,128,128]{2,1,0:T(8,128)(2,1)S(1)}, u32[]{:S(2)}, u32[]{:S(2)}) async-start(bf16[16,128,128]{2,1,0:T(8,128)(2,1)} %prefix.4), calls=%async_computation.4 | async-start | bytes 1048576 | tf_op jit(solution)/shard_map/all_to_all | solution.py:402
  156.5 8.1 %copy-start.8 = (bf16[16,128,128]{2,1,0:T(8,128)(2,1)}, bf16[16,128,128]{2,1,0:T(8,128)(2,1)S(1)}, u32[]{:S(2)}) copy-start(bf16[16,128,128]{2,1,0:T(8,128)(2,1)S(1)} %all-to-all-done.4) | copy-start | bytes 1572868
  156.5 19.1 %all-to-all-start.2 = ((bf16[16,128,128]{2,1,0:T(8,128)(2,1)}), bf16[16,128,128]{2,1,0:T(8,128)(2,1)S(1)}, u32[]{:S(2)}, u32[]{:S(2)}) async-start(bf16[16,128,128]{2,1,0:T(8,128)(2,1)} %prefix.3), calls=%async_computation.2 | async-start | bytes 1048576 | tf_op jit(solution)/shard_map/all_to_all | solution.py:402
  163.0 59.5 %collective-permute-start.6 = (bf16[2048,128]{1,0:T(8,128)(2,1)}, bf16[2048,128]{1,0:T(8,128)(2,1)S(1)}, u32[]{:S(2)}, u32[]{:S(2)}) collective-permute-start(bf16[2048,128]{1,0:T(8,128)(2,1)} %get-tuple-element.73), channel_id=1, source_target_pairs={{0,1},{1,0},{2,3},{3,2},{4,5},{5,4},{6,7},{7,6},{8,9},{9,8},{10,11... | collective-permute-start | bytes 1572872 | tf_op jit(solution)/shard_map/ppermute | solution.py:398
  167.3 55.2 %collective-permute-start.4 = (bf16[2048,128]{1,0:T(8,128)(2,1)}, bf16[2048,128]{1,0:T(8,128)(2,1)S(1)}, u32[]{:S(2)}, u32[]{:S(2)}) collective-permute-start(bf16[2048,128]{1,0:T(8,128)(2,1)} %get-tuple-element.69), channel_id=1, source_target_pairs={{0,1},{1,0},{2,3},{3,2},{4,5},{5,4},{6,7},{7,6},{8,9},{9,8},{10,11... | collective-permute-start | bytes 1572872 | tf_op jit(solution)/shard_map/ppermute | solution.py:398
  175.6 0.8 copy-start.6
  179.2 43.4 %collective-permute-start.2 = (bf16[2048,128]{1,0:T(8,128)(2,1)}, bf16[2048,128]{1,0:T(8,128)(2,1)S(1)}, u32[]{:S(2)}, u32[]{:S(2)}) collective-permute-start(bf16[2048,128]{1,0:T(8,128)(2,1)} %get-tuple-element.65), channel_id=1, source_target_pairs={{0,1},{1,0},{2,3},{3,2},{4,5},{5,4},{6,7},{7,6},{8,9},{9,8},{10,11... | collective-permute-start | bytes 1572872 | tf_op jit(solution)/shard_map/ppermute | solution.py:398
  222.5 0.8 copy-start.11
  222.5 1.0 copy-start.12
  222.6 1.2 copy-start.13
